TPU v7x, 32 devices: a whole 2x2x4 slice. The times are simulated.
32 devices in a mesh: dp: 8 (over y, x, core), chan: 4 (over z).
Axes of the slice: x: 2, y: 2, z: 4, core: 2. Of those that a mesh axis runs over, the one named last changes fastest.
Arguments:
- inputs: bfloat16 [192, 152, 800], P('dp', None, 'chan'), may hold values from -6 to 6
- ocean_mask: int32 [192, 152], P('dp'), may hold values 0 or 1
- counts: int32 [4], replicated, may hold values from 1 to 2
- kernel: float32 [7, 7, 800], P(None, None, 'chan'), may hold values from -0.875 to 0.875
- conv_bias: float32 [800], P('chan'), may hold values from -3 to 3
- norm_gain: float32 [800], P('chan'), may hold values from 0.5 to 1.5
- norm_bias: float32 [800], P('chan'), may hold values from -3 to 3
- weight_in: bfloat16 [800, 3200], P(None, 'chan'), may hold values from -0.21875 to 0.21875
- bias_in: float32 [3200], P('chan'), may hold values from -3 to 3
- weight_out: bfloat16 [3200, 800], P('chan'), may hold values from -0.21875 to 0.21875
- bias_out: float32 [800], P('chan'), may hold values from -3 to 3
- cotangent: bfloat16 [192, 152, 800], P('dp', None, 'chan'), may hold values from -6 to 6
Outputs:
- output: bfloat16 [192, 152, 800], P('dp', None, 'chan')
- grad_inputs: float32 [192, 152, 800], P('dp', None, 'chan')
- grad_kernel: float32 [7, 7, 800], P(None, None, 'chan')
- grad_conv_bias: float32 [800], P('chan')
- grad_gain: float32 [800], P('chan')
- grad_norm_bias: float32 [800], P('chan')
- grad_weight_in: float32 [800, 3200], P(None, 'chan')
- grad_bias_in: float32 [3200], P('chan')
- grad_weight_out: float32 [3200, 800], P('chan')
- grad_bias_out: float32 [800], P('chan')
All inputs are finite; a program needn't handle non-finite values. No bound on the sum of `ocean_mask` on one device may be relied on, other than what follows from the above.
Results may differ from a plain program's by a relative error of at most 0.0057.
Values may be sent and summed in bfloat16 or wider, within the bound.
No kernel may reach another device: no remote copies, remote signals or barrier semaphores. Data moves between devices by JAX's collectives and lax.ppermute only.
A program may use at most 192 MiB of HBM per device.

v0:
```python
import jax
import jax.numpy as jnp
from jax import lax
from jax.sharding import PartitionSpec as P

CH = 800
GROUPS = 8
HISTORY = 2
SPAN = 2
EPSILON = 1e-05


def swapped(block, axis, distance):
    count = lax.axis_size(axis)
    route = []
    for low in range(count):
        high = low | 1 << distance
        if high != low and high < count:
            route += [(low, high), (high, low)]
    return lax.ppermute(block, axis, route)


def with_rim(values, rim, top_valid, bottom_valid):
    return jnp.concatenate([rim * top_valid, values, rim * bottom_valid], axis=0)


def local_groups(values, group_size):
    height, across, local_ch = values.shape
    return jnp.sum(
        values.reshape(height, across, local_ch // group_size, group_size), axis=(0, 1, 3)
    )


def spread_groups(summed, group_size, members):
    return jnp.repeat(summed, group_size) / members


def gelu_slope(hidden):
    cumulative = 0.5 * (1.0 + lax.erf(hidden * 0.7071067811865476))
    density = jnp.exp(-0.5 * hidden * hidden) * 0.3989422804014327
    return cumulative + hidden * density


def body(
    inputs,
    ocean_mask,
    counts,
    kernel,
    conv_bias,
    norm_gain,
    norm_bias,
    weight_in,
    bias_in,
    weight_out,
    bias_out,
    cotangent,
):
    height, across, local_ch = inputs.shape
    pixels = height * across
    group_size = CH // GROUPS
    members = height * SPAN * across * group_size
    dp_index = lax.axis_index("dp")
    sample = dp_index // SPAN
    within = dp_index % SPAN
    sample_ids = jnp.arange(counts.shape[0])
    count_here = jnp.sum(jnp.where(sample_ids == sample, counts, 0))
    channel = lax.axis_index("chan") * local_ch + jnp.arange(local_ch)
    history_keep = (channel // (CH // HISTORY) < count_here).astype(jnp.float32)
    wet_cells = ocean_mask.astype(jnp.float32)[:, :, None]
    masked = inputs.astype(jnp.float32) * wet_cells * history_keep
    top_valid = (within > 0).astype(jnp.float32)
    bottom_valid = (within == 0).astype(jnp.float32)
    is_upper = within == 0
    masked_low = masked.astype(jnp.bfloat16)
    outgoing = jnp.where(is_upper, masked_low[height - 3 :], masked_low[:3])
    rim_in = swapped(outgoing, "dp", 0).astype(jnp.float32)
    padded = jnp.pad(with_rim(masked, rim_in, top_valid, bottom_valid), ((0, 0), (3, 3), (0, 0)))
    convolved = jnp.zeros((height, across, local_ch), jnp.float32) + conv_bias
    for row_shift in range(7):
        for col_shift in range(7):
            convolved = (
                convolved
                + padded[row_shift : row_shift + height, col_shift : col_shift + across]
                * kernel[row_shift, col_shift]
            )
    own_sum = local_groups(convolved, group_size)
    centre = spread_groups(own_sum + swapped(own_sum, "dp", 0), group_size, members)
    offset = convolved - centre
    own_sq = local_groups(offset * offset, group_size)
    spread = spread_groups(own_sq + swapped(own_sq, "dp", 0), group_size, members)
    inverse = lax.rsqrt(spread + EPSILON)
    standard = offset * inverse
    normed = (standard * norm_gain + norm_bias).astype(jnp.bfloat16).reshape(pixels, local_ch)
    grad_res = cotangent.astype(jnp.float32) * wet_cells
    grad_branch = grad_res.reshape(pixels, local_ch).astype(jnp.bfloat16)
    grad_bias_out = jnp.sum(grad_branch.astype(jnp.float32), 0)
    gathered = lax.all_gather(normed, "chan", axis=1, tiled=True)
    hidden = jnp.dot(gathered, weight_in, preferred_element_type=jnp.float32) + bias_in
    active = jax.nn.gelu(hidden, approximate=False).astype(jnp.bfloat16)
    partial_value = jnp.dot(active, weight_out, preferred_element_type=jnp.float32)
    branch = lax.psum_scatter(partial_value, "chan", scatter_dimension=1, tiled=True) + bias_out
    output = (wet_cells * (masked + branch.reshape(height, across, local_ch))).astype(jnp.bfloat16)
    grad_gathered = lax.all_gather(grad_branch, "chan", axis=1, tiled=True)
    grad_active = lax.dot_general(
        grad_gathered, weight_out, (((1,), (1,)), ((), ())), preferred_element_type=jnp.float32
    )
    grad_weight_out = lax.dot_general(
        active, grad_gathered, (((0,), (0,)), ((), ())), preferred_element_type=jnp.float32
    )
    grad_hidden = (grad_active * gelu_slope(hidden)).astype(jnp.bfloat16)
    grad_bias_in = jnp.sum(grad_hidden.astype(jnp.float32), 0)
    grad_weight_in = lax.dot_general(
        gathered, grad_hidden, (((0,), (0,)), ((), ())), preferred_element_type=jnp.float32
    )
    grad_part = lax.dot_general(
        grad_hidden, weight_in, (((1,), (1,)), ((), ())), preferred_element_type=jnp.float32
    )
    grad_normed = lax.psum_scatter(grad_part, "chan", scatter_dimension=1, tiled=True).reshape(
        height, across, local_ch
    )
    grad_gain = jnp.sum(grad_normed * standard, (0, 1))
    grad_norm_bias = jnp.sum(grad_normed, (0, 1))
    grad_standard = grad_normed * norm_gain
    own_pair = jnp.stack(
        [
            local_groups(grad_standard, group_size),
            local_groups(grad_standard * standard, group_size),
        ]
    )
    both_pair = own_pair + swapped(own_pair, "dp", 0)
    mean_first = spread_groups(both_pair[0], group_size, members)
    mean_second = spread_groups(both_pair[1], group_size, members)
    grad_conv = inverse * (grad_standard - mean_first - standard * mean_second)
    grad_conv_bias = jnp.sum(grad_conv, (0, 1))
    kernel_rows = []
    for row_shift in range(7):
        for col_shift in range(7):
            kernel_rows.append(
                jnp.sum(
                    grad_conv
                    * padded[row_shift : row_shift + height, col_shift : col_shift + across],
                    (0, 1),
                )
            )
    grad_kernel = jnp.stack(kernel_rows).reshape(7, 7, local_ch)
    grad_out_rows = jnp.where(is_upper, grad_conv[height - 3 :], grad_conv[:3])
    grad_rim = swapped(grad_out_rows.astype(jnp.bfloat16), "dp", 0).astype(grad_out_rows.dtype)
    grad_padded = jnp.pad(
        with_rim(grad_conv, grad_rim, top_valid, bottom_valid), ((0, 0), (3, 3), (0, 0))
    )
    grad_masked = jnp.zeros((height, across, local_ch), jnp.float32)
    for row_shift in range(7):
        for col_shift in range(7):
            grad_masked = (
                grad_masked
                + grad_padded[
                    6 - row_shift : 6 - row_shift + height, 6 - col_shift : 6 - col_shift + across
                ]
                * kernel[row_shift, col_shift]
            )
    grad_inputs = wet_cells * history_keep * (grad_res + grad_masked)
    (
        grad_kernel,
        grad_conv_bias,
        grad_gain,
        grad_norm_bias,
        grad_weight_in,
        grad_bias_in,
        grad_weight_out,
        grad_bias_out,
    ) = lax.psum(
        (
            grad_kernel,
            grad_conv_bias,
            grad_gain,
            grad_norm_bias,
            grad_weight_in,
            grad_bias_in,
            grad_weight_out,
            grad_bias_out,
        ),
        "dp",
    )
    return (
        output,
        grad_inputs,
        grad_kernel,
        grad_conv_bias,
        grad_gain,
        grad_norm_bias,
        grad_weight_in,
        grad_bias_in,
        grad_weight_out,
        grad_bias_out,
    )


def solution(mesh):
    in_specs = (
        P("dp", None, "chan"),
        P("dp", None),
        P(),
        P(None, None, "chan"),
        P("chan"),
        P("chan"),
        P("chan"),
        P(None, "chan"),
        P("chan"),
        P("chan", None),
        P("chan"),
        P("dp", None, "chan"),
    )
    out_specs = (
        P("dp", None, "chan"),
        P("dp", None, "chan"),
        P(None, None, "chan"),
        P("chan"),
        P("chan"),
        P("chan"),
        P(None, "chan"),
        P("chan"),
        P("chan", None),
        P("chan"),
    )
    return jax.shard_map(body, mesh=mesh, in_specs=in_specs, out_specs=out_specs, check_vma=False)
```

profile of v0, /device:TPU:0, one launch (start us, length us, event | category | flops | bytes accessed | tf_op | source)
XLA Modules:
  0.0 971.4 jit_solution(3660102376321455770)
XLA Ops:
  10.1 5.1 convert_reduce_fusion.1
  17.4 4.5 select_maximum_fusion.2
  22.3 75.7 %fusion.88 = (f32[200]{0:T(256)S(1)}, f32[24,152,200]{2,1,0:T(8,128)}) fusion(f32[200]{0:T(256)} %bitcast.48, f32[30,158,200]{2,1,0:T(8,128)} %select_maximum_fusion.2, f32[200]{0:T(256)} %bitcast.47, f32[200]{0:T(256)S(1)} %bitcast.130, f32[200]{0:T(256)S(1)} %bitcast.132, f32[3,152,200]{2,1,0:T(8,128)S(1)} %get-tuple-element.86, ...), kind=kLoop, calls=%fused_computation.242 | loop fusion | flops 76607800 | bytes 129180000 | tf_op jit(solution)/shard_map/reduce_sum | solution.py:29
  99.5 2.6 multiply_reduce_fusion.51
  103.7 2.7 add_convert_fusion
  106.4 2.5 copy.31
  108.9 3.8 copy.33
  112.9 108.1 %all-gather.3.cloned.1.call-done = bf16[3648,800]{0,1:T(8,128)(2,1)} async-done(((bf16[3648,200]{0,1:T(8,128)(2,1)}), bf16[3648,800]{0,1:T(8,128)(2,1)}) %all-gather.3.cloned.1.call-update) | async-done | bytes 5836816 | tf_op jit(solution)/shard_map/all_gather | solution.py:97
  221.0 35.8 %fusion.2 = (bf16[3648,800]{0,1:T(8,128)(2,1)}, f32[3648,800]{0,1:T(8,128)}) fusion(f32[800]{0:T(1024)S(1)} %copy-done.101, bf16[3648,800]{0,1:T(8,128)(2,1)} %all-gather.3.cloned.1.call-done, bf16[800,800]{1,0:T(8,128)(2,1)S(1)} %copy-done), kind=kOutput, calls=%fused_computation.4 | convolution fusion | flops 4862054400 | bytes 24630400 | tf_op jit(solution)/shard_map/dot_general | solution.py:98
  256.8 74.2 %all-gather.5.cloned.1.call-done = bf16[3648,800]{0,1:T(8,128)(2,1)} async-done(((bf16[3648,200]{0,1:T(8,128)(2,1)}), bf16[3648,800]{0,1:T(8,128)(2,1)}) %all-gather.5.cloned.1.call-update) | async-done | bytes 5836816 | tf_op jit(solution)/shard_map/all_gather | solution.py:103
  331.0 12.0 %convert_reduce_fusion = (f32[800]{0:T(1024)S(1)}, bf16[3648,800]{0,1:T(8,128)(2,1)S(1)}) fusion(f32[3648,800]{0,1:T(8,128)} %get-tuple-element.141, f32[800]{0:T(1024)S(1)} %copy-done.101, bf16[800,800]{1,0:T(8,128)(2,1)} %param.21, bf16[3648,800]{0,1:T(8,128)(2,1)} %all-gather.5.cloned.1.call-done), kind=kOutput, calls=%fused_computation.11 | convolution fusion | flops 4707378176 | bytes 24633600 | tf_op jit(solution)/shard_map/dot_general | solution.py:104
  343.1 2.6 copy-done.102
  345.6 9.2 fusion.95
  356.2 11.5 %fusion.92 = f32[3648,800]{0,1:T(8,128)} fusion(bf16[3648,800]{0,1:T(8,128)(2,1)} %get-tuple-element.140, bf16[800,800]{1,0:T(8,128)(2,1)S(1)} %copy-done.100), kind=kOutput, calls=%fused_computation.246 | convolution fusion | flops 4669440000 | bytes 18790400 | tf_op jit(solution)/shard_map/dot_general | solution.py:100
  367.8 11.4 %fusion.94 = f32[800,800]{1,0:T(8,128)} fusion(bf16[3648,800]{0,1:T(8,128)(2,1)} %get-tuple-element.140, bf16[3648,800]{0,1:T(8,128)(2,1)} %all-gather.5.cloned.1.call-done), kind=kOutput, calls=%fused_computation.248 | convolution fusion | flops 4669440000 | bytes 14233600 | tf_op jit(solution)/shard_map/dot_general | solution.py:107
  379.2 11.5 %fusion.93 = f32[800,800]{1,0:T(8,128)} fusion(bf16[3648,800]{0,1:T(8,128)(2,1)} %all-gather.3.cloned.1.call-done, bf16[3648,800]{0,1:T(8,128)(2,1)} %copy-done.102), kind=kOutput, calls=%fused_computation.247 | convolution fusion | flops 4669440000 | bytes 14233600 | tf_op jit(solution)/shard_map/dot_general | solution.py:112
  390.7 164.1 %reduce-scatter.9.cloned.1.call-done = f32[3648,200]{0,1:T(8,128)} async-done(((f32[3648,800]{0,1:T(8,128)}), f32[3648,200]{0,1:T(8,128)}) %reduce-scatter.9.cloned.1.call-update) | async-done | bytes 2918416
  554.8 2.3 fusion.86
  557.3 4.9 copy.34
  562.2 5.3 multiply_reduce_fusion
  567.8 191.2 %reduce-scatter.7.cloned.1.call-done = f32[3648,200]{0,1:T(8,128)} async-done(((f32[3648,800]{0,1:T(8,128)}), f32[3648,200]{0,1:T(8,128)}) %reduce-scatter.7.cloned.1.call-update) | async-done | bytes 2918416
  759.0 4.9 copy.32
  763.9 4.1 broadcast_add_fusion
  768.4 38.1 %multiply_reduce_fusion.1 = (f32[200]{0:T(256)S(1)}, f32[200]{0:T(256)S(1)}, f32[200]{0:T(256)S(1)}, f32[200]{0:T(256)S(1)}, f32[200]{0:T(256)S(1)}, /*index=5*/...) fusion(f32[30,158,200]{2,1,0:T(8,128)} %select_maximum_fusion.2, ...), kind=kLoop, calls=%fused_computation.162 | loop fusion | flops 31369200 | bytes 61304800 | tf_op jit(solution)/shard_map/reduce_sum | solution.py:139
  806.6 30.1 %multiply_reduce_fusion.2 = (f32[200]{0:T(256)S(1)}, f32[200]{0:T(256)S(1)}, f32[200]{0:T(256)S(1)}, f32[200]{0:T(256)S(1)}, f32[200]{0:T(256)S(1)}, /*index=5*/...) fusion(f32[24,152,200]{2,1,0:T(8,128)} %get-tuple-element.77, ...), kind=kLoop, calls=%fused_computation.163 | loop fusion | flops 26262000 | bytes 55464000 | tf_op jit(solution)/shard_map/reduce_sum | solution.py:139
  836.8 8.8 multiply_reduce_fusion.4
  845.6 3.4 multiply_reduce_fusion.43
  849.2 26.3 %all-reduce.4 = (f32[7,7,200]{2,1,0:T(8,128)}, f32[200]{0:T(256)}, f32[200]{0:T(256)}, f32[200]{0:T(256)}, f32[800]{0:T(1024)}, /*index=5*/f32[200]{0:T(256)}) all-reduce(f32[7,7,200]{2,1,0:T(8,128)S(1)} %reshape.110, f32[200]{0:T(256)S(1)} %get-tuple-element.63, ...), channel_id=1, replica_groups=mesh['dp'=8,'chan'=4] {'dp'}, use_global_device_ids=true, to_apply=%region_60.61 | all-reduce | flops 11400 | bytes 91200 | tf_op jit(solution)/shard_map/psum | solution.py:171
  876.0 4.5 select_maximum_fusion
  880.9 78.5 %fusion.31 = f32[24,152,200]{2,1,0:T(8,128)} fusion(f32[24,152,200]{2,1,0:T(8,128)} %get-tuple-element.77, f32[3,152,200]{2,1,0:T(8,128)S(1)} %get-tuple-element.84, f32[3,152,200]{2,1,0:T(8,128)S(1)} %get-tuple-element.83, f32[30,158,200]{2,1,0:T(8,128)} %select_maximum_fusion, bf16[24,152,200]{2,1,0:T(8,128)(2,1)S(1)} %copy-done.5, f32[200]{0:T(256)} %bitcast.48, ...), kind=kLoop, calls=%fused_computation.64 | loop fusion | flops 78796800 | bytes 130652992 | tf_op jit(solution)/shard_map/mul | solution.py:161
  959.4 3.7 copy.37
  963.1 1.6 copy.38
  (264 shorter events, 11.0 us)
Async XLA Ops:
  7.2 213.8 %copy-start = (bf16[800,800]{1,0:T(8,128)(2,1)S(1)}, bf16[800,800]{1,0:T(8,128)(2,1)}, u32[]{:S(2)}) copy-start(bf16[800,800]{1,0:T(8,128)(2,1)} %param.19) | copy-start | bytes 3840004
  7.2 213.8 %all-gather.3.cloned.1.call-start = ((), (), s32[]{:S(2)}) async-start(), calls=%async_computation.2 | async-start | bytes 7424000 | tf_op jit(solution)/shard_map/all_gather | solution.py:97
  8.1 7.1 copy-start.11
  15.2 2.1 collective-permute-start
  15.7 6.2 copy-start.22
  15.7 6.1 copy-start.24
  15.7 6.1 copy-start.26
  15.8 6.1 copy-start.28
  15.8 6.1 copy-start.30
  15.8 6.1 copy-start.32
  15.8 6.1 copy-start.34
  98.2 1.2 collective-permute-start.1
  99.5 6.8 copy-start.14
  102.3 1.2 collective-permute-start.2
  108.8 112.2 %copy-start.101 = (f32[800]{0:T(1024)S(1)}, f32[800]{0:T(1024)}, u32[]{:S(2)}) copy-start(f32[800]{0:T(1024)} %param.20) | copy-start | bytes 9604
  108.8 222.2 %all-gather.5.cloned.1.call-start = ((), (), s32[]{:S(2)}) async-start(), calls=%async_computation.3 | async-start | bytes 7424000 | tf_op jit(solution)/shard_map/all_gather | solution.py:103
  112.7 442.1 %reduce-scatter.9.cloned.1.call-start = ((), (), s32[]{:S(2)}) async-start(), calls=%async_computation.5 | async-start | bytes 14848000
  354.9 404.1 %reduce-scatter.7.cloned.1.call-start = ((), (), s32[]{:S(2)}) async-start(), calls=%async_computation.4 | async-start | bytes 14848000
  367.8 591.6 %all-reduce.8.cloned.1.call-start = ((), (), s32[]{:S(2)}) async-start(), calls=%async_computation.6 | async-start | bytes 11468800 | tf_op jit(solution)/shard_map/psum | solution.py:171
  390.7 164.1 %copy-start.17 = (f32[200]{0:T(256)S(1)}, f32[200]{0:T(256)}, u32[]{:S(2)}) copy-start(f32[200]{0:T(256)} %param.17) | copy-start | bytes 2404
  567.5 196.4 %copy-start.98 = (f32[200]{0:T(256)S(1)}, f32[200]{0:T(256)}, u32[]{:S(2)}) copy-start(f32[200]{0:T(256)} %param.22) | copy-start | bytes 2404
  567.7 200.3 %collective-permute-start.3 = (f32[2,2]{1,0:T(2,128)S(1)}, f32[2,2]{1,0:T(2,128)S(1)}, u32[]{:S(2)}, u32[]{:S(2)}) collective-permute-start(f32[2,2]{1,0:T(2,128)S(1)} %pad_maximum_fusion.4), channel_id=1, source_target_pairs={{0,4},{4,0},{8,12},{12,8},{16,20},{20,16},{24,28},{28,24},{1,5},{5... | collective-permute-start | bytes 56 | tf_op jit(solution)/shard_map/ppermute | solution.py:20
  768.4 77.2 %slice-start = ((s8[4915200]{0:T(1024)(128)(4,1)}), s8[720896]{0:T(1024)(128)(4,1)S(1)}, s32[]{:S(2)}) async-start(s8[4915200]{0:T(1024)(128)(4,1)} %bitcast.121), calls=%async_computation.7 | async-start | bytes 1441792
  806.5 30.1 %copy-start.2 = (f32[24,152,200]{2,1,0:T(8,128)S(1)}, f32[24,152,200]{2,1,0:T(8,128)}, u32[]{:S(2)}) copy-start(f32[24,152,200]{2,1,0:T(8,128)} %get-tuple-element.77) | copy-start | bytes 8755204
  806.5 30.2 %copy-start.3 = (f32[24,152,200]{2,1,0:T(8,128)S(1)}, f32[24,152,200]{2,1,0:T(8,128)}, u32[]{:S(2)}) copy-start(f32[24,152,200]{2,1,0:T(8,128)} %get-tuple-element.137) | copy-start | bytes 8755204
  806.5 30.2 %copy-start.4 = (bf16[24,152,200]{2,1,0:T(8,128)(2,1)S(1)}, bf16[24,152,200]{2,1,0:T(8,128)(2,1)}, u32[]{:S(2)}) copy-start(bf16[24,152,200]{2,1,0:T(8,128)(2,1)} %param.12) | copy-start | bytes 4377604
  806.5 30.2 %copy-start.7 = (f32[3,152,200]{2,1,0:T(8,128)S(1)}, f32[3,152,200]{2,1,0:T(8,128)}, u32[]{:S(2)}) copy-start(f32[3,152,200]{2,1,0:T(8,128)} %copy-done.6) | copy-start | bytes 1094404
  806.5 30.2 %copy-start.9 = (f32[3,152,200]{2,1,0:T(8,128)S(1)}, f32[3,152,200]{2,1,0:T(8,128)}, u32[]{:S(2)}) copy-start(f32[3,152,200]{2,1,0:T(8,128)} %copy-done.8) | copy-start | bytes 1094404
  806.6 30.2 %copy-start.12 = (f32[24,152]{1,0:T(8,128)S(1)}, f32[24,152]{1,0:T(8,128)}, u32[]{:S(2)}) copy-start(f32[24,152]{1,0:T(8,128)} %copy-done.11) | copy-start | bytes 43780
  806.6 30.2 %copy-start.21 = (f32[200]{0:T(256)S(1)}, f32[200]{0:T(256)}, u32[]{:S(2)}) copy-start(f32[200]{0:T(256)} %copy-done.20) | copy-start | bytes 2404
  806.6 39.0 %slice-start.1 = ((s8[4915200]{0:T(1024)(128)(4,1)}), s8[4194304]{0:T(1024)(128)(4,1)S(1)}, s32[]{:S(2)}) async-start(s8[4915200]{0:T(1024)(128)(4,1)} %bitcast.121), calls=%async_computation.8 | async-start | bytes 8388608
  845.6 30.0 %collective-permute-start.4 = (bf16[3,152,200]{2,1,0:T(8,128)(2,1)S(1)}, bf16[3,152,200]{2,1,0:T(8,128)(2,1)S(1)}, u32[]{:S(2)}, u32[]{:S(2)}) collective-permute-start(bf16[3,152,200]{2,1,0:T(8,128)(2,1)S(1)} %fusion.83), channel_id=1, source_target_pairs={{0,4},{4,0},{8,12},{12,8},{16,20},{20,16},{24,28},{28,24},{1,5},{5... | collective-permute-start | bytes 547208 | tf_op jit(solution)/shard_map/ppermute | solution.py:20
  (83 other events, 427.6 us)
Sparse Core Ops, SparseCore 0:
  109.0 111.9 all-gather.2
  223.1 107.8 all-gather.4
  355.0 199.7 reduce-scatter.8
  557.0 201.9 reduce-scatter.6
  763.4 99.3 all-reduce.7
where the time goes:
time: 979 us; the launch traced here: 971 us
  waiting for transfers between devices  540 us (55%)
  other arithmetic  269 us (27%)
  matrix products  91.5 us (9%)
  local copies, waits for them, and re-layouts  27.8 us (3%)
  blocking collectives  26.3 us (3%)
  between operations  15.6 us (2%)
    unnamed x7, waiting for transfers between devices  355 us
    all_gather x1, waiting for transfers between devices, body(): gathered = lax.all_gather(normed, 'chan', axis=1, tiled=True)  108 us
    reduce_sum x4, other arithmetic, body(): jnp.sum(grad_conv * padded[row_shift:row_shift + height, col_shift:col_sh...  80.4 us
    reduce_sum x6, other arithmetic, local_groups(): jnp.sum(values.reshape(height, across, local_ch // group_size, group_size...  78.8 us
    mul x1, other arithmetic, body(): grad_inputs = wet_cells * history_keep * (grad_res + grad_masked)  78.5 us
    all_gather x1, waiting for transfers between devices, body(): grad_gathered = lax.all_gather(grad_branch, 'chan', axis=1, tiled=True)  74.2 us
    dot_general x1, matrix products, body(): jnp.dot(gathered, weight_in, preferred_element_type=jnp.float32) + bias_in  35.8 us
    psum x1, blocking collectives, body(): lax.psum((grad_kernel, grad_conv_bias, grad_gain, grad_norm_bias, grad_we...  26.3 us
  transfers between devices with their start and end apart: 10, of which 6 were waited for; matrix products, arithmetic and copies ran while one was open for 27% of the time, Pallas kernels for 0%

commit v1 on v0

--- a/solution.py
+++ b/solution.py
@@ -94,7 +94,27 @@
     grad_res = cotangent.astype(jnp.float32) * wet_cells
     grad_branch = grad_res.reshape(pixels, local_ch).astype(jnp.bfloat16)
     grad_bias_out = jnp.sum(grad_branch.astype(jnp.float32), 0)
-    gathered = lax.all_gather(normed, "chan", axis=1, tiled=True)
+    prior = lax.axis_size("chan")
+    main = lax.axis_index("chan")
+    far_arr, block_last, reply = (prior, main, normed.shape[1])
+    sheets = [(dev, (dev + 1) % far_arr) for dev in range(far_arr)]
+    heap = [(dev, (dev - 1) % far_arr) for dev in range(far_arr)]
+    gathered = jnp.zeros((*normed.shape[:1], far_arr * reply, *normed.shape[2:]), normed.dtype)
+    gathered = lax.dynamic_update_slice_in_dim(gathered, normed, block_last * reply, axis=1)
+    arr_now = o_now = normed
+    val2 = far_arr // 2
+    pp = 1
+    while pp < val2 + 1:
+        arr_now = lax.ppermute(arr_now, "chan", sheets)
+        gathered = lax.dynamic_update_slice_in_dim(
+            gathered, arr_now, (block_last - pp) % far_arr * reply, axis=1
+        )
+        if pp < far_arr - val2:
+            o_now = lax.ppermute(o_now, "chan", heap)
+            gathered = lax.dynamic_update_slice_in_dim(
+                gathered, o_now, (block_last + pp) % far_arr * reply, axis=1
+            )
+        pp += 1
     hidden = jnp.dot(gathered, weight_in, preferred_element_type=jnp.float32) + bias_in
     active = jax.nn.gelu(hidden, approximate=False).astype(jnp.bfloat16)
     partial_value = jnp.dot(active, weight_out, preferred_element_type=jnp.float32)

time: 979 us -> 914 us (0.934)
  waiting for transfers between devices: 540 us -> 455 us
    all_gather x1 -> x0, waiting for transfers between devices: 108 us -> none  [body(): gathered = lax.all_gather(normed, 'chan', axis=1, tiled=True)]
    ppermute x0 -> x3, waiting for transfers between devices: none -> 98.1 us  [the longest x2 75.9 us: body(): arr_now = lax.ppermute(arr_now, 'chan', sheets)]
    all_gather x1, waiting for transfers between devices: 74.2 us -> 0.01 us  [body(): grad_gathered = lax.all_gather(grad_branch, 'chan', axis=1, tiled=True)]
    unnamed x7 -> x6, waiting for transfers between devices: 355 us -> 355 us
  transfers between devices with their start and end apart: 10 -> 12, of which waited for: 6 -> 7; matrix products, arithmetic and copies ran while one was open for 27% -> 36% of each run, Pallas kernels for 0% -> 0%
where the time goes in v1:
time: 914 us; the launch traced here: 907 us
  waiting for transfers between devices  455 us (50%)
  other arithmetic  270 us (30%)
  matrix products  95.4 us (10%)
  local copies, waits for them, and re-layouts  37.4 us (4%)
  blocking collectives  26.4 us (3%)
  between operations  15.8 us (2%)
    unnamed x6, waiting for transfers between devices  355 us
    reduce_sum x4, other arithmetic, body(): jnp.sum(grad_conv * padded[row_shift:row_shift + height, col_shift:col_sh...  80.2 us
    reduce_sum x6, other arithmetic, local_groups(): jnp.sum(values.reshape(height, across, local_ch // group_size, group_size...  78.8 us
    mul x1, other arithmetic, body(): grad_inputs = wet_cells * history_keep * (grad_res + grad_masked)  78.5 us
    ppermute x2, waiting for transfers between devices, body(): arr_now = lax.ppermute(arr_now, 'chan', sheets)  75.9 us
    dot_general x1, matrix products, body(): jnp.dot(gathered, weight_in, preferred_element_type=jnp.float32) + bias_in  42.4 us
    psum x1, blocking collectives, body(): lax.psum((grad_kernel, grad_conv_bias, grad_gain, grad_norm_bias, grad_we...  26.4 us
    ppermute x1, waiting for transfers between devices, body(): o_now = lax.ppermute(o_now, 'chan', heap)  22.2 us
  transfers between devices with their start and end apart: 12, of which 7 were waited for; matrix products, arithmetic and copies ran while one was open for 36% of the time, Pallas kernels for 0%

profile of v1, /device:TPU:0, one launch (start us, length us, event | category | flops | bytes accessed | tf_op | source)
XLA Modules:
  0.0 906.6 jit_solution(15635170377378346630)
XLA Ops:
  10.1 5.1 convert_reduce_fusion.1
  20.9 4.5 select_maximum_fusion.2
  25.8 75.7 %fusion.89 = (f32[200]{0:T(256)S(1)}, f32[24,152,200]{2,1,0:T(8,128)}) fusion(f32[200]{0:T(256)} %bitcast.48, f32[30,158,200]{2,1,0:T(8,128)} %select_maximum_fusion.2, f32[200]{0:T(256)} %bitcast.47, f32[200]{0:T(256)S(1)} %bitcast.130, f32[200]{0:T(256)S(1)} %bitcast.132, f32[3,152,200]{2,1,0:T(8,128)S(1)} %get-tuple-element.89, ...), kind=kLoop, calls=%fused_computation.246 | loop fusion | flops 76607800 | bytes 129180000 | tf_op jit(solution)/shard_map/reduce_sum | solution.py:29
  103.1 2.6 multiply_reduce_fusion.51
  107.3 2.7 add_convert_fusion
  112.4 2.8 collective-permute-start.3
  117.3 44.5 %collective-permute-done.3 = bf16[3648,200]{0,1:T(8,128)(2,1)} collective-permute-done((bf16[3648,200]{0,1:T(8,128)(2,1)}, bf16[3648,200]{0,1:T(8,128)(2,1)}, u32[]{:S(2)}, u32[]{:S(2)}) %collective-permute-start.3) | collective-permute-done | bytes 1459232 | tf_op jit(solution)/shard_map/ppermute | solution.py:108
  162.0 3.0 broadcast_in_dim.15
  166.2 2.7 constant_dynamic-update-slice_fusion.2
  169.0 22.2 %collective-permute-done.4 = bf16[3648,200]{0,1:T(8,128)(2,1)} collective-permute-done((bf16[3648,200]{0,1:T(8,128)(2,1)}, bf16[3648,200]{0,1:T(8,128)(2,1)}, u32[]{:S(2)}, u32[]{:S(2)}) %collective-permute-start.4) | collective-permute-done | bytes 1459232 | tf_op jit(solution)/shard_map/ppermute | solution.py:113
  191.1 2.6 constant_dynamic-update-slice_fusion.1
  193.8 31.4 %collective-permute-done.5 = bf16[3648,200]{0,1:T(8,128)(2,1)S(1)} collective-permute-done((bf16[3648,200]{0,1:T(8,128)(2,1)}, bf16[3648,200]{0,1:T(8,128)(2,1)S(1)}, u32[]{:S(2)}, u32[]{:S(2)}) %collective-permute-start.5) | collective-permute-done | bytes 1459232 | tf_op jit(solution)/shard_map/ppermute | solution.py:108
  226.4 9.2 %fusion.96 = f32[3648,800]{0,1:T(8,128)S(1)} fusion(bf16[800,800]{1,0:T(8,128)(2,1)S(1)} %copy-done.101, bf16[3648,800]{0,1:T(8,128)(2,1)} %all-gather.2.cloned.1.call-done), kind=kOutput, calls=%fused_computation.253 | convolution fusion | flops 4669440000 | bytes 18790400 | tf_op jit(solution)/shard_map/dot_general | solution.py:124
  235.6 42.4 %convert_reduce_fusion = (f32[800]{0:T(1024)S(1)}, bf16[3648,800]{0,1:T(8,128)(2,1)S(1)}, bf16[3648,800]{0,1:T(8,128)(2,1)}) fusion(f32[3648,800]{0,1:T(8,128)S(1)} %fusion.96, f32[800]{0:T(1024)S(1)} %copy-done.103, bf16[3648,800]{0,1:T(8,128)(2,1)} %constant_dynamic-update-slice_fusion, bf16[800,800]{1,0:T(8,128)(2,1)S(1)} %copy-done), kind=kOutput, calls=%fused_computation.11 | convolution fusion | flops 4897074176 | bytes 30470400 | tf_op jit(solution)/shard_map/dot_general | solution.py:118
  280.5 9.3 %fusion.97 = f32[3648,800]{0,1:T(8,128)} fusion(bf16[800,800]{1,0:T(8,128)(2,1)S(1)} %copy-done, bf16[3648,800]{0,1:T(8,128)(2,1)S(1)} %get-tuple-element.78), kind=kOutput, calls=%fused_computation.254 | convolution fusion | flops 4669440000 | bytes 18790400 | tf_op jit(solution)/shard_map/dot_general | solution.py:135
  291.1 11.6 %fusion.93 = f32[3648,800]{0,1:T(8,128)} fusion(bf16[3648,800]{0,1:T(8,128)(2,1)} %get-tuple-element.82, bf16[800,800]{1,0:T(8,128)(2,1)S(1)} %copy-done.102), kind=kOutput, calls=%fused_computation.250 | convolution fusion | flops 4669440000 | bytes 18790400 | tf_op jit(solution)/shard_map/dot_general | solution.py:120
  302.8 11.4 %fusion.94 = f32[800,800]{1,0:T(8,128)} fusion(bf16[3648,800]{0,1:T(8,128)(2,1)} %constant_dynamic-update-slice_fusion, bf16[3648,800]{0,1:T(8,128)(2,1)} %copy-done.104), kind=kOutput, calls=%fused_computation.251 | convolution fusion | flops 4669440000 | bytes 14233600 | tf_op jit(solution)/shard_map/dot_general | solution.py:132
  314.2 11.4 %fusion.95 = f32[800,800]{1,0:T(8,128)} fusion(bf16[3648,800]{0,1:T(8,128)(2,1)} %get-tuple-element.82, bf16[3648,800]{0,1:T(8,128)(2,1)} %all-gather.2.cloned.1.call-done), kind=kOutput, calls=%fused_computation.252 | convolution fusion | flops 4669440000 | bytes 14233600 | tf_op jit(solution)/shard_map/dot_general | solution.py:127
  325.7 163.8 %reduce-scatter.9.cloned.1.call-done = f32[3648,200]{0,1:T(8,128)} async-done(((f32[3648,800]{0,1:T(8,128)}), f32[3648,200]{0,1:T(8,128)}) %reduce-scatter.9.cloned.1.call-update) | async-done | bytes 2918416
  492.0 4.9 copy.38
  496.9 5.3 multiply_reduce_fusion
  502.5 191.4 %reduce-scatter.7.cloned.1.call-done = f32[3648,200]{0,1:T(8,128)} async-done(((f32[3648,800]{0,1:T(8,128)}), f32[3648,200]{0,1:T(8,128)}) %reduce-scatter.7.cloned.1.call-update) | async-done | bytes 2918416
  693.9 4.9 copy.36
  698.8 4.1 broadcast_add_fusion
  703.3 37.9 %multiply_reduce_fusion.1 = (f32[200]{0:T(256)S(1)}, f32[200]{0:T(256)S(1)}, f32[200]{0:T(256)S(1)}, f32[200]{0:T(256)S(1)}, f32[200]{0:T(256)S(1)}, /*index=5*/...) fusion(f32[30,158,200]{2,1,0:T(8,128)} %select_maximum_fusion.2, ...), kind=kLoop, calls=%fused_computation.162 | loop fusion | flops 31369200 | bytes 61304800 | tf_op jit(solution)/shard_map/reduce_sum | solution.py:159
  741.3 30.1 %multiply_reduce_fusion.2 = (f32[200]{0:T(256)S(1)}, f32[200]{0:T(256)S(1)}, f32[200]{0:T(256)S(1)}, f32[200]{0:T(256)S(1)}, f32[200]{0:T(256)S(1)}, /*index=5*/...) fusion(f32[24,152,200]{2,1,0:T(8,128)} %get-tuple-element.79, ...), kind=kLoop, calls=%fused_computation.163 | loop fusion | flops 26262000 | bytes 55464000 | tf_op jit(solution)/shard_map/reduce_sum | solution.py:159
  771.6 8.8 multiply_reduce_fusion.4
  780.4 3.4 multiply_reduce_fusion.43
  784.0 26.4 %all-reduce.4 = (f32[7,7,200]{2,1,0:T(8,128)}, f32[200]{0:T(256)}, f32[200]{0:T(256)}, f32[200]{0:T(256)}, f32[800]{0:T(1024)}, /*index=5*/f32[200]{0:T(256)}) all-reduce(f32[7,7,200]{2,1,0:T(8,128)S(1)} %reshape.110, f32[200]{0:T(256)S(1)} %get-tuple-element.63, ...), channel_id=1, replica_groups=mesh['dp'=8,'chan'=4] {'dp'}, use_global_device_ids=true, to_apply=%region_60.61 | all-reduce | flops 11400 | bytes 91200 | tf_op jit(solution)/shard_map/psum | solution.py:191
  810.9 4.5 select_maximum_fusion
  815.7 78.5 %fusion.31 = f32[24,152,200]{2,1,0:T(8,128)} fusion(f32[24,152,200]{2,1,0:T(8,128)} %get-tuple-element.79, f32[3,152,200]{2,1,0:T(8,128)S(1)} %get-tuple-element.87, f32[3,152,200]{2,1,0:T(8,128)S(1)} %get-tuple-element.86, f32[30,158,200]{2,1,0:T(8,128)} %select_maximum_fusion, bf16[24,152,200]{2,1,0:T(8,128)(2,1)S(1)} %copy-done.5, f32[200]{0:T(256)} %bitcast.48, ...), kind=kLoop, calls=%fused_computation.64 | loop fusion | flops 78796800 | bytes 130652992 | tf_op jit(solution)/shard_map/mul | solution.py:181
  894.3 3.7 copy.45
  (276 shorter events, 27.9 us)
Async XLA Ops:
  7.2 228.4 %copy-start = (bf16[800,800]{1,0:T(8,128)(2,1)S(1)}, bf16[800,800]{1,0:T(8,128)(2,1)}, u32[]{:S(2)}) copy-start(bf16[800,800]{1,0:T(8,128)(2,1)} %param.19) | copy-start | bytes 3840004
  7.2 219.2 %all-gather.2.cloned.1.call-start = ((), (), s32[]{:S(2)}) async-start(), calls=%async_computation.2 | async-start | bytes 7424000 | tf_op jit(solution)/shard_map/all_gather | solution.py:123
  8.1 7.0 copy-start.12
  17.6 471.9 %reduce-scatter.9.cloned.1.call-start = ((), (), s32[]{:S(2)}) async-start(), calls=%async_computation.4 | async-start | bytes 14848000
  18.8 2.1 collective-permute-start
  19.3 6.2 copy-start.23
  19.3 6.1 copy-start.25
  19.3 6.1 copy-start.27
  101.8 1.2 collective-permute-start.1
  103.1 6.8 copy-start.15
  105.9 1.2 collective-permute-start.2
  112.4 52.6 %copy-start.10 = (bf16[3648,200]{0,1:T(8,128)(2,1)S(1)}, bf16[3648,200]{0,1:T(8,128)(2,1)}, u32[]{:S(2)}) copy-start(bf16[3648,200]{0,1:T(8,128)(2,1)} %copy.33) | copy-start | bytes 4377604
  112.4 49.4 %collective-permute-start.3 = (bf16[3648,200]{0,1:T(8,128)(2,1)}, bf16[3648,200]{0,1:T(8,128)(2,1)}, u32[]{:S(2)}, u32[]{:S(2)}) collective-permute-start(bf16[3648,200]{0,1:T(8,128)(2,1)} %copy.33), channel_id=1, source_target_pairs={{0,1},{1,2},{2,3},{3,0},{4,5},{5,6},{6,7},{7,4},{8,9},{9,10},{10,1... | collective-permute-start | bytes 4377608 | tf_op jit(solution)/shard_map/ppermute | solution.py:108
  115.2 76.0 %collective-permute-start.4 = (bf16[3648,200]{0,1:T(8,128)(2,1)}, bf16[3648,200]{0,1:T(8,128)(2,1)}, u32[]{:S(2)}, u32[]{:S(2)}) collective-permute-start(bf16[3648,200]{0,1:T(8,128)(2,1)} %copy.33), channel_id=1, source_target_pairs={{0,3},{1,0},{2,1},{3,2},{4,7},{5,4},{6,5},{7,6},{8,11},{9,8},{10,9... | collective-permute-start | bytes 4377608 | tf_op jit(solution)/shard_map/ppermute | solution.py:113
  161.8 63.4 %collective-permute-start.5 = (bf16[3648,200]{0,1:T(8,128)(2,1)}, bf16[3648,200]{0,1:T(8,128)(2,1)S(1)}, u32[]{:S(2)}, u32[]{:S(2)}) collective-permute-start(bf16[3648,200]{0,1:T(8,128)(2,1)} %collective-permute-done.3), channel_id=1, source_target_pairs={{0,1},{1,2},{2,3},{3,0},{4,5},{5,6},{6,7},{7,4},{8,9},{9,10},{10,1... | collective-permute-start | bytes 4377608 | tf_op jit(solution)/shard_map/ppermute | solution.py:108
  166.2 60.2 %copy-start.101 = (bf16[800,800]{1,0:T(8,128)(2,1)S(1)}, bf16[800,800]{1,0:T(8,128)(2,1)}, u32[]{:S(2)}) copy-start(bf16[800,800]{1,0:T(8,128)(2,1)} %param.21) | copy-start | bytes 3840004
  226.4 9.2 %copy-start.103 = (f32[800]{0:T(1024)S(1)}, f32[800]{0:T(1024)}, u32[]{:S(2)}) copy-start(f32[800]{0:T(1024)} %param.20) | copy-start | bytes 9604
  289.8 404.1 %reduce-scatter.7.cloned.1.call-start = ((), (), s32[]{:S(2)}) async-start(), calls=%async_computation.3 | async-start | bytes 14848000
  302.8 591.5 %all-reduce.8.cloned.1.call-start = ((), (), s32[]{:S(2)}) async-start(), calls=%async_computation.5 | async-start | bytes 11468800 | tf_op jit(solution)/shard_map/psum | solution.py:191
  325.7 163.9 %copy-start.18 = (f32[200]{0:T(256)S(1)}, f32[200]{0:T(256)}, u32[]{:S(2)}) copy-start(f32[200]{0:T(256)} %param.17) | copy-start | bytes 2404
  502.2 196.6 %copy-start.99 = (f32[200]{0:T(256)S(1)}, f32[200]{0:T(256)}, u32[]{:S(2)}) copy-start(f32[200]{0:T(256)} %param.22) | copy-start | bytes 2404
  502.4 200.5 %collective-permute-start.6 = (f32[2,2]{1,0:T(2,128)S(1)}, f32[2,2]{1,0:T(2,128)S(1)}, u32[]{:S(2)}, u32[]{:S(2)}) collective-permute-start(f32[2,2]{1,0:T(2,128)S(1)} %pad_maximum_fusion.4), channel_id=1, source_target_pairs={{0,4},{4,0},{8,12},{12,8},{16,20},{20,16},{24,28},{28,24},{1,5},{5... | collective-permute-start | bytes 56 | tf_op jit(solution)/shard_map/ppermute | solution.py:20
  703.3 77.1 %slice-start = ((s8[4915200]{0:T(1024)(128)(4,1)}), s8[720896]{0:T(1024)(128)(4,1)S(1)}, s32[]{:S(2)}) async-start(s8[4915200]{0:T(1024)(128)(4,1)} %bitcast.121), calls=%async_computation.6 | async-start | bytes 1441792
  741.2 30.1 %copy-start.2 = (f32[24,152,200]{2,1,0:T(8,128)S(1)}, f32[24,152,200]{2,1,0:T(8,128)}, u32[]{:S(2)}) copy-start(f32[24,152,200]{2,1,0:T(8,128)} %get-tuple-element.79) | copy-start | bytes 8755204
  741.2 30.3 %copy-start.3 = (f32[24,152,200]{2,1,0:T(8,128)S(1)}, f32[24,152,200]{2,1,0:T(8,128)}, u32[]{:S(2)}) copy-start(f32[24,152,200]{2,1,0:T(8,128)} %get-tuple-element.140) | copy-start | bytes 8755204
  741.2 30.3 %copy-start.4 = (bf16[24,152,200]{2,1,0:T(8,128)(2,1)S(1)}, bf16[24,152,200]{2,1,0:T(8,128)(2,1)}, u32[]{:S(2)}) copy-start(bf16[24,152,200]{2,1,0:T(8,128)(2,1)} %param.12) | copy-start | bytes 4377604
  741.2 30.3 %copy-start.7 = (f32[3,152,200]{2,1,0:T(8,128)S(1)}, f32[3,152,200]{2,1,0:T(8,128)}, u32[]{:S(2)}) copy-start(f32[3,152,200]{2,1,0:T(8,128)} %copy-done.6) | copy-start | bytes 1094404
  741.3 30.3 %copy-start.9 = (f32[3,152,200]{2,1,0:T(8,128)S(1)}, f32[3,152,200]{2,1,0:T(8,128)}, u32[]{:S(2)}) copy-start(f32[3,152,200]{2,1,0:T(8,128)} %copy-done.8) | copy-start | bytes 1094404
  741.3 30.3 %copy-start.13 = (f32[24,152]{1,0:T(8,128)S(1)}, f32[24,152]{1,0:T(8,128)}, u32[]{:S(2)}) copy-start(f32[24,152]{1,0:T(8,128)} %copy-done.12) | copy-start | bytes 43780
  741.3 30.3 %copy-start.22 = (f32[200]{0:T(256)S(1)}, f32[200]{0:T(256)}, u32[]{:S(2)}) copy-start(f32[200]{0:T(256)} %copy-done.21) | copy-start | bytes 2404
  741.3 39.1 %slice-start.1 = ((s8[4915200]{0:T(1024)(128)(4,1)}), s8[4194304]{0:T(1024)(128)(4,1)S(1)}, s32[]{:S(2)}) async-start(s8[4915200]{0:T(1024)(128)(4,1)} %bitcast.121), calls=%async_computation.7 | async-start | bytes 8388608
  771.4 39.0 %collective-permute-start.7 = (bf16[3,152,200]{2,1,0:T(8,128)(2,1)S(1)}, bf16[3,152,200]{2,1,0:T(8,128)(2,1)S(1)}, u32[]{:S(2)}, u32[]{:S(2)}) collective-permute-start(bf16[3,152,200]{2,1,0:T(8,128)(2,1)S(1)} %fusion.83), channel_id=1, source_target_pairs={{0,4},{4,0},{8,12},{12,8},{16,20},{20,16},{24,28},{28,24},{1,5},{5... | collective-permute-start | bytes 547208 | tf_op jit(solution)/shard_map/ppermute | solution.py:20
  (87 other events, 450.5 us)
Sparse Core Ops, SparseCore 0:
  17.7 150.7 all-gather.1
  289.9 199.5 reduce-scatter.8
  491.9 201.9 reduce-scatter.6
  698.3 99.3 all-reduce.7
